TPU v7x, 128 devices: a whole 4x4x4 slice. The times are simulated.
128 devices in a mesh: blk: 8 (over x_lo, y), row: 16 (over x_hi, z, core).
Axes of the slice: x: 4 (x_hi: 2, x_lo: 2; x = x_hi * 2 + x_lo), y: 4, z: 4, core: 2. Of those that a mesh axis runs over, the one named last changes fastest.
Arguments:
- intersection: bfloat16 [4096, 4096], P('row', 'blk'), may hold values from -0.09375 to 0.09375
- inverse_dev: bfloat16 [4096, 4096], P('row', 'blk'), may hold values from -0.09375 to 0.09375
- hamiltonian: bfloat16 [4096, 4096], P('row', 'blk'), may hold values from -0.0625 to 0.0625
- chem_potential: float32 [1], replicated, may hold values from -0.4 to 0.4
- pattern_s: int32 [32, 32], replicated, may hold values 0 or 1
- pattern_z: int32 [32, 32], replicated, may hold values 0 or 1
- pattern_h: int32 [32, 32], replicated, may hold values 0 or 1
- fill_inverse: int32 [32, 32], replicated, may hold values 0 or 1
- fill_sign: int32 [32, 32], replicated, may hold values 0 or 1
Outputs:
- refined_inverse: bfloat16 [4096, 4096], P('row', 'blk')
- inverse_error: bfloat16 [4096, 4096], P('row', 'blk')
- sign_step: bfloat16 [4096, 4096], P('row', 'blk')
All inputs are finite; a program needn't handle non-finite values.
Results may differ from a plain program's by a relative error of at most 0.0067.
Values may be sent and summed in bfloat16 or wider, within the bound.
No kernel may reach another device: no remote copies, remote signals or barrier semaphores. Data moves between devices by JAX's collectives and lax.ppermute only.
A program may use at most 64 MiB of HBM per device.

v0:
```python
import jax
import jax.numpy as jnp
from jax import lax
from jax.sharding import PartitionSpec as P

BS = 128


def expand_local(pattern, row_start, rows, col_start, cols):
    count = pattern.shape[0]
    labels = jnp.arange(count, dtype=jnp.int32)
    row_blocks = (row_start + jnp.arange(rows, dtype=jnp.int32)) // BS
    col_blocks = (col_start + jnp.arange(cols, dtype=jnp.int32)) // BS
    row_pick = (row_blocks[:, None] == labels[None, :]).astype(jnp.float32)
    col_pick = (col_blocks[:, None] == labels[None, :]).astype(jnp.float32)
    inner = jnp.dot(row_pick, pattern.astype(jnp.float32), precision=lax.Precision.HIGHEST)
    return jnp.dot(inner, col_pick.T, precision=lax.Precision.HIGHEST)


def make_folder(panel, piece):
    return jnp.dot(panel, piece, preferred_element_type=jnp.float32)


def body(
    intersection,
    inverse_dev,
    hamiltonian,
    chem_potential,
    pattern_s,
    pattern_z,
    pattern_h,
    fill_inverse,
    fill_sign,
):
    rows, cols = intersection.shape
    row_start = lax.axis_index("row") * rows
    col_start = lax.axis_index("blk") * cols
    ident = (
        (row_start + jnp.arange(rows, dtype=jnp.int32))[:, None]
        == (col_start + jnp.arange(cols, dtype=jnp.int32))[None, :]
    ).astype(jnp.float32)
    seff = (
        ident
        + 0.35
        * expand_local(pattern_s, row_start, rows, col_start, cols)
        * intersection.astype(jnp.float32)
    ).astype(jnp.bfloat16)
    zeff = (
        ident
        - 0.35
        * expand_local(pattern_z, row_start, rows, col_start, cols)
        * inverse_dev.astype(jnp.float32)
    ).astype(jnp.bfloat16)
    heff = (
        expand_local(pattern_h, row_start, rows, col_start, cols) * hamiltonian.astype(jnp.float32)
    ).astype(jnp.bfloat16)
    z_rows = lax.all_gather(zeff, "blk", axis=1, tiled=True)
    s_cols = lax.all_gather(seff, "row", axis=0, tiled=True)
    first = jnp.dot(z_rows, s_cols, preferred_element_type=jnp.float32).astype(jnp.bfloat16)
    f_rows = lax.all_gather(first, "blk", axis=1, tiled=True)
    second = make_folder(f_rows, lax.all_gather(zeff, "row", axis=0, tiled=True))
    keep_inverse = expand_local(fill_inverse, row_start, rows, col_start, cols)
    refined = (keep_inverse * (2.0 * zeff.astype(jnp.float32) - second)).astype(jnp.bfloat16)
    r_rows = lax.all_gather(refined, "blk", axis=1, tiled=True)
    error = (ident - jnp.dot(r_rows, s_cols, preferred_element_type=jnp.float32)).astype(
        jnp.bfloat16
    )
    third = make_folder(r_rows, lax.all_gather(heff, "row", axis=0, tiled=True))
    keep_sign = expand_local(fill_sign, row_start, rows, col_start, cols)
    shifted = (keep_sign * third - chem_potential[0] * ident).astype(jnp.bfloat16)
    x_rows = lax.all_gather(shifted, "blk", axis=1, tiled=True)
    squared = make_folder(x_rows, lax.all_gather(shifted, "row", axis=0, tiled=True))
    square = (keep_sign * squared).astype(jnp.bfloat16)
    cube = make_folder(x_rows, lax.all_gather(square, "row", axis=0, tiled=True))
    sign = (0.5 * (3.0 * shifted.astype(jnp.float32) - cube)).astype(jnp.bfloat16)
    return (refined, error, sign)


def solution(mesh):
    placed = (P("row", "blk"), P("row", "blk"), P("row", "blk"), P(), P(), P(), P(), P(), P())
    return jax.shard_map(
        body,
        mesh=mesh,
        in_specs=placed,
        out_specs=(P("row", "blk"), P("row", "blk"), P("row", "blk")),
        check_vma=False,
    )
```

profile of v0, /device:TPU:1, one launch (start us, length us, event | category | flops | bytes accessed | tf_op | source)
XLA Modules:
  0.0 479.5 jit_solution(4841761674206644709)
XLA Ops:
  7.2 0.0 all-gather.10.cloned.1.call-start
  7.3 1.0 fusion.23
  8.3 2.2 fusion.10
  10.5 0.0 all-gather.10.cloned.1.call-update
  10.5 0.0 all-gather.12.cloned.1.call-start
  10.5 1.0 fusion.22
  11.5 2.2 fusion.9
  13.7 0.0 all-gather.12.cloned.1.call-update
  13.7 0.0 copy-start.2
  13.7 0.0 all-gather.16.cloned.1.call-start
  13.8 0.7 all-gather.16.cloned.1.call-update
  14.5 0.0 copy-start.4
  14.5 0.0 copy-start
  14.5 0.0 all-gather.14.cloned.1.call-start
  14.5 35.2 %all-gather.10.cloned.1.call-done = bf16[256,4096]{1,0:T(8,128)(2,1)} async-done(((bf16[256,512]{1,0:T(8,128)(2,1)}), bf16[256,4096]{1,0:T(8,128)(2,1)}) %all-gather.10.cloned.1.call-update) | async-done | bytes 2097168 | tf_op jit(solution)/shard_map/all_gather | solution.py:57
  49.7 63.2 %all-gather.12.cloned.1.call-done = bf16[4096,512]{1,0:T(8,128)(2,1)} async-done(((bf16[256,512]{1,0:T(8,128)(2,1)}), bf16[4096,512]{1,0:T(8,128)(2,1)}) %all-gather.12.cloned.1.call-update) | async-done | bytes 4194320 | tf_op jit(solution)/shard_map/all_gather | solution.py:58
  112.9 4.8 convolution_convert_fusion
  117.7 0.0 all-gather.14.cloned.1.call-update
  117.7 0.0 all-gather.20.cloned.1.call-start
  117.7 0.0 copy-done.3
  117.8 0.3 fusion.20
  118.0 1.2 fusion.12
  119.3 0.0 all-gather.20.cloned.1.call-update
  119.3 0.0 all-gather.18.cloned.1.call-start
  119.3 0.3 fusion.24
  119.6 0.0 copy-start.5
  119.6 49.1 %all-gather.16.cloned.1.call-done = bf16[4096,512]{1,0:T(8,128)(2,1)} async-done(((bf16[256,512]{1,0:T(8,128)(2,1)}), bf16[4096,512]{1,0:T(8,128)(2,1)}) %all-gather.16.cloned.1.call-update) | async-done | bytes 4194320 | tf_op jit(solution)/shard_map/all_gather | solution.py:61
  168.7 35.3 %all-gather.14.cloned.1.call-done = bf16[256,4096]{1,0:T(8,128)(2,1)} async-done(((bf16[256,512]{1,0:T(8,128)(2,1)}), bf16[256,4096]{1,0:T(8,128)(2,1)}) %all-gather.14.cloned.1.call-update) | async-done | bytes 2097168 | tf_op jit(solution)/shard_map/all_gather | solution.py:60
  204.0 4.1 convolution_subtract_fusion.2
  208.1 1.2 fusion.11
  209.3 0.0 all-gather.18.cloned.1.call-update
  209.3 0.0 all-gather.22.cloned.1.call-start
  210.0 0.3 fusion.21
  210.3 0.5 fusion.14
  210.8 55.7 %all-gather.20.cloned.1.call-done = bf16[4096,512]{1,0:T(8,128)(2,1)} async-done(((bf16[256,512]{1,0:T(8,128)(2,1)}), bf16[4096,512]{1,0:T(8,128)(2,1)}) %all-gather.20.cloned.1.call-update) | async-done | bytes 4194320 | tf_op jit(solution)/shard_map/all_gather | solution.py:68
  266.5 35.3 %all-gather.18.cloned.1.call-done = bf16[256,4096]{1,0:T(8,128)(2,1)} async-done(((bf16[256,512]{1,0:T(8,128)(2,1)}), bf16[256,4096]{1,0:T(8,128)(2,1)}) %all-gather.18.cloned.1.call-update) | async-done | bytes 2097168 | tf_op jit(solution)/shard_map/all_gather | solution.py:64
  301.8 4.8 fusion.6
  306.6 0.0 all-gather.22.cloned.1.call-update
  306.6 0.0 all-gather.24.cloned.1.call-start
  306.7 0.7 all-gather.24.cloned.1.call-update
  307.4 0.0 all-gather.26.cloned.1.call-start
  307.4 40.0 %all-gather.22.cloned.1.call-done = bf16[256,4096]{1,0:T(8,128)(2,1)} async-done(((bf16[256,512]{1,0:T(8,128)(2,1)}), bf16[256,4096]{1,0:T(8,128)(2,1)}) %all-gather.22.cloned.1.call-update) | async-done | bytes 2097168 | tf_op jit(solution)/shard_map/all_gather | solution.py:71
  347.4 63.2 %all-gather.24.cloned.1.call-done = bf16[4096,512]{1,0:T(8,128)(2,1)} async-done(((bf16[256,512]{1,0:T(8,128)(2,1)}), bf16[4096,512]{1,0:T(8,128)(2,1)}) %all-gather.24.cloned.1.call-update) | async-done | bytes 4194320 | tf_op jit(solution)/shard_map/all_gather | solution.py:72
  410.5 4.8 fusion.13
  415.3 0.0 all-gather.26.cloned.1.call-update
  415.4 4.2 fusion.7
  419.6 48.6 %all-gather.26.cloned.1.call-done = bf16[4096,512]{1,0:T(8,128)(2,1)} async-done(((bf16[256,512]{1,0:T(8,128)(2,1)}), bf16[4096,512]{1,0:T(8,128)(2,1)}) %all-gather.26.cloned.1.call-update) | async-done | bytes 4194320 | tf_op jit(solution)/shard_map/all_gather | solution.py:74
  468.2 4.8 fusion.8
  (13 shorter events, 0.0 us)
Async XLA Ops:
  7.2 42.6 %all-gather.10.cloned.1.call-start = ((), (), s32[]{:S(2)}) async-start(), calls=%async_computation | async-start | bytes 2359296 | tf_op jit(solution)/shard_map/all_gather | solution.py:57
  10.5 102.4 %all-gather.12.cloned.1.call-start = ((), (), s32[]{:S(2)}) async-start(), calls=%async_computation.1 | async-start | bytes 4456448 | tf_op jit(solution)/shard_map/all_gather | solution.py:58
  13.7 104.0 %copy-start.3 = (s32[32,32]{1,0:T(8,128)S(1)}, s32[32,32]{1,0:T(8,128)}, u32[]{:S(2)}) copy-start(s32[32,32]{1,0:T(8,128)} %param.15) | copy-start | bytes 12292
  13.7 104.3 %copy-start.2 = (bf16[256,512]{1,0:T(8,128)(2,1)S(1)}, bf16[256,512]{1,0:T(8,128)(2,1)}, u32[]{:S(2)}) copy-start(bf16[256,512]{1,0:T(8,128)(2,1)} %param.11) | copy-start | bytes 786436
  13.7 155.0 %all-gather.16.cloned.1.call-start = ((), (), s32[]{:S(2)}) async-start(), calls=%async_computation.3 | async-start | bytes 4456448 | tf_op jit(solution)/shard_map/all_gather | solution.py:61
  14.5 104.9 %copy-start.4 = (s32[32,32]{1,0:T(8,128)S(1)}, s32[32,32]{1,0:T(8,128)}, u32[]{:S(2)}) copy-start(s32[32,32]{1,0:T(8,128)} %param.16) | copy-start | bytes 12292
  14.5 189.5 %copy-start = (bf16[256,512]{1,0:T(8,128)(2,1)S(1)}, bf16[256,512]{1,0:T(8,128)(2,1)}, u32[]{:S(2)}) copy-start(bf16[256,512]{1,0:T(8,128)(2,1)} %fusion.10) | copy-start | bytes 786436
  14.5 189.5 %all-gather.14.cloned.1.call-start = ((), (), s32[]{:S(2)}) async-start(), calls=%async_computation.2 | async-start | bytes 2359296 | tf_op jit(solution)/shard_map/all_gather | solution.py:60
  117.7 148.8 %all-gather.20.cloned.1.call-start = ((), (), s32[]{:S(2)}) async-start(), calls=%async_computation.5 | async-start | bytes 4456448 | tf_op jit(solution)/shard_map/all_gather | solution.py:68
  119.3 182.5 %all-gather.18.cloned.1.call-start = ((), (), s32[]{:S(2)}) async-start(), calls=%async_computation.4 | async-start | bytes 2359296 | tf_op jit(solution)/shard_map/all_gather | solution.py:64
  119.6 90.4 %copy-start.5 = (s32[32,32]{1,0:T(8,128)S(1)}, s32[32,32]{1,0:T(8,128)}, u32[]{:S(2)}) copy-start(s32[32,32]{1,0:T(8,128)} %param.17) | copy-start | bytes 12292
  209.3 138.1 %all-gather.22.cloned.1.call-start = ((), (), s32[]{:S(2)}) async-start(), calls=%async_computation.6 | async-start | bytes 2359296 | tf_op jit(solution)/shard_map/all_gather | solution.py:71
  306.6 108.8 %copy-start.6 = (bf16[256,4096]{1,0:T(8,128)(2,1)S(1)}, bf16[256,4096]{1,0:T(8,128)(2,1)}, u32[]{:S(2)}) copy-start(bf16[256,4096]{1,0:T(8,128)(2,1)} %all-gather.18.cloned.1.call-done) | copy-start | bytes 6291460
  306.6 103.9 %all-gather.24.cloned.1.call-start = ((), (), s32[]{:S(2)}) async-start(), calls=%async_computation.7 | async-start | bytes 4456448 | tf_op jit(solution)/shard_map/all_gather | solution.py:72
  307.4 160.9 %all-gather.26.cloned.1.call-start = ((), (), s32[]{:S(2)}) async-start(), calls=%async_computation.8 | async-start | bytes 4456448 | tf_op jit(solution)/shard_map/all_gather | solution.py:74
  415.3 52.9 %copy-start.1 = (bf16[256,512]{1,0:T(8,128)(2,1)S(1)}, bf16[256,512]{1,0:T(8,128)(2,1)}, u32[]{:S(2)}) copy-start(bf16[256,512]{1,0:T(8,128)(2,1)} %fusion.6) | copy-start | bytes 786436
Sparse Core Ops, SparseCore 0:
  10.6 39.0 all-gather.9
  52.8 60.0 all-gather.11
  115.9 52.6 all-gather.15
  170.8 33.2 all-gather.13
  206.3 60.0 all-gather.19
  268.5 33.2 all-gather.17
  306.7 40.6 all-gather.21
  350.4 60.0 all-gather.23
  415.5 52.6 all-gather.25
where the time goes:
time: 480 us
  waiting for transfers between devices  427 us (89%)
  matrix products  37.4 us (8%)
  between operations  14.7 us (3%)
    all_gather x1, waiting for transfers between devices, body(): s_cols = lax.all_gather(seff, 'row', axis=0, tiled=True)  63.2 us
    all_gather x1, waiting for transfers between devices, body(): lax.all_gather(shifted, 'row', axis=0, tiled=True)  63.2 us
    all_gather x1, waiting for transfers between devices, body(): third = make_folder(r_rows, lax.all_gather(heff, 'row', axis=0, tiled=True))  55.7 us
    all_gather x1, waiting for transfers between devices, body(): lax.all_gather(zeff, 'row', axis=0, tiled=True)  49.1 us
    all_gather x1, waiting for transfers between devices, body(): lax.all_gather(square, 'row', axis=0, tiled=True)  48.6 us
    all_gather x1, waiting for transfers between devices, body(): x_rows = lax.all_gather(shifted, 'blk', axis=1, tiled=True)  40 us
    all_gather x1, waiting for transfers between devices, body(): f_rows = lax.all_gather(first, 'blk', axis=1, tiled=True)  35.3 us
    all_gather x1, waiting for transfers between devices, body(): r_rows = lax.all_gather(refined, 'blk', axis=1, tiled=True)  35.3 us
  transfers between devices with their start and end apart: 9, of which 9 were waited for; matrix products, arithmetic and copies ran while one was open for 4% of the time, Pallas kernels for 0%

commit v1 on v0

--- a/solution.py
+++ b/solution.py
@@ -57,7 +57,9 @@
     z_rows = lax.all_gather(zeff, "blk", axis=1, tiled=True)
     s_cols = lax.all_gather(seff, "row", axis=0, tiled=True)
     first = jnp.dot(z_rows, s_cols, preferred_element_type=jnp.float32).astype(jnp.bfloat16)
-    f_rows = lax.all_gather(first, "blk", axis=1, tiled=True)
+    f_rows = jnp.concatenate(
+        lax.all_to_all(jnp.stack([first] * lax.axis_size("blk")), "blk", 0, 0), axis=1
+    )
     second = make_folder(f_rows, lax.all_gather(zeff, "row", axis=0, tiled=True))
     keep_inverse = expand_local(fill_inverse, row_start, rows, col_start, cols)
     refined = (keep_inverse * (2.0 * zeff.astype(jnp.float32) - second)).astype(jnp.bfloat16)

time: 480 us -> 441 us (0.919)
  waiting for transfers between devices: 427 us -> 381 us
    all_gather x1 -> x0, waiting for transfers between devices: 35.3 us -> none  [body(): f_rows = lax.all_gather(first, 'blk', axis=1, tiled=True)]
    all_gather x1, waiting for transfers between devices: 55.7 us -> 48.9 us  [body(): third = make_folder(r_rows, lax.all_gather(heff, 'row', axis=0, tiled=True))]
  transfers between devices with their start and end apart: 9 -> 9, of which waited for: 9 -> 8; matrix products, arithmetic and copies ran while one was open for 4% -> 5% of each run, Pallas kernels for 0% -> 0%
where the time goes in v1:
time: 441 us; the launch traced here: 440 us
  waiting for transfers between devices  381 us (86%)
  matrix products  37.8 us (9%)
  between operations  14.9 us (3%)
    all_gather x1, waiting for transfers between devices, body(): s_cols = lax.all_gather(seff, 'row', axis=0, tiled=True)  63.2 us
    all_gather x1, waiting for transfers between devices, body(): lax.all_gather(shifted, 'row', axis=0, tiled=True)  63.2 us
    all_gather x1, waiting for transfers between devices, body(): third = make_folder(r_rows, lax.all_gather(heff, 'row', axis=0, tiled=True))  48.9 us
    all_gather x1, waiting for transfers between devices, body(): lax.all_gather(zeff, 'row', axis=0, tiled=True)  48.8 us
    all_gather x1, waiting for transfers between devices, body(): lax.all_gather(square, 'row', axis=0, tiled=True)  48.6 us
    all_gather x1, waiting for transfers between devices, body(): x_rows = lax.all_gather(shifted, 'blk', axis=1, tiled=True)  40 us
    all_gather x1, waiting for transfers between devices, body(): r_rows = lax.all_gather(refined, 'blk', axis=1, tiled=True)  35.3 us
    all_gather x1, waiting for transfers between devices, body(): z_rows = lax.all_gather(zeff, 'blk', axis=1, tiled=True)  32 us
  transfers between devices with their start and end apart: 9, of which 8 were waited for; matrix products, arithmetic and copies ran while one was open for 5% of the time, Pallas kernels for 0%

profile of v1, /device:TPU:1, one launch (start us, length us, event | category | flops | bytes accessed | tf_op | source)
XLA Modules:
  0.0 440.1 jit_solution(10017777731580842221)
XLA Ops:
  7.2 0.0 all-gather.9.cloned.1.call-start
  7.3 1.0 fusion.23
  8.3 2.2 fusion.10
  10.5 0.0 all-gather.9.cloned.1.call-update
  10.5 0.0 all-gather.11.cloned.1.call-start
  10.5 1.0 fusion.22
  11.5 2.2 fusion.9
  13.7 0.0 all-gather.11.cloned.1.call-update
  13.7 0.0 all-gather.13.cloned.1.call-start
  13.8 0.7 all-gather.13.cloned.1.call-update
  14.5 0.0 all-gather.17.cloned.1.call-start
  14.5 1.0 fusion.20
  15.5 2.2 fusion.12
  17.7 0.0 all-gather.17.cloned.1.call-update
  17.7 32.0 %all-gather.9.cloned.1.call-done = bf16[256,4096]{1,0:T(8,128)(2,1)} async-done(((bf16[256,512]{1,0:T(8,128)(2,1)}), bf16[256,4096]{1,0:T(8,128)(2,1)}) %all-gather.9.cloned.1.call-update) | async-done | bytes 2097168 | tf_op jit(solution)/shard_map/all_gather | solution.py:57
  49.7 63.2 %all-gather.11.cloned.1.call-done = bf16[4096,512]{1,0:T(8,128)(2,1)} async-done(((bf16[256,512]{1,0:T(8,128)(2,1)}), bf16[4096,512]{1,0:T(8,128)(2,1)}) %all-gather.11.cloned.1.call-update) | async-done | bytes 4194320 | tf_op jit(solution)/shard_map/all_gather | solution.py:58
  112.9 4.1 convolution_convert_fusion
  117.0 0.0 copy-start.2
  117.0 0.0 copy-start
  117.0 0.1 copy.12
  117.1 1.4 stack.2
  118.6 4.0 all-to-all-start
  122.6 0.0 all-gather.15.cloned.1.call-start
  122.6 0.3 fusion.24
  122.9 48.8 %all-gather.13.cloned.1.call-done = bf16[4096,512]{1,0:T(8,128)(2,1)} async-done(((bf16[256,512]{1,0:T(8,128)(2,1)}), bf16[4096,512]{1,0:T(8,128)(2,1)}) %all-gather.13.cloned.1.call-update) | async-done | bytes 4194320 | tf_op jit(solution)/shard_map/all_gather | solution.py:63
  171.7 0.0 all-to-all-done
  171.7 0.0 copy-done
  171.7 3.5 convolution_subtract_fusion.2
  175.2 1.2 fusion.11
  176.4 0.0 all-gather.15.cloned.1.call-update
  176.4 0.0 all-gather.19.cloned.1.call-start
  177.1 0.0 copy-done.3
  177.1 0.3 fusion.21
  177.4 0.5 fusion.14
  177.8 48.9 %all-gather.17.cloned.1.call-done = bf16[4096,512]{1,0:T(8,128)(2,1)} async-done(((bf16[256,512]{1,0:T(8,128)(2,1)}), bf16[4096,512]{1,0:T(8,128)(2,1)}) %all-gather.17.cloned.1.call-update) | async-done | bytes 4194320 | tf_op jit(solution)/shard_map/all_gather | solution.py:70
  226.7 35.3 %all-gather.15.cloned.1.call-done = bf16[256,4096]{1,0:T(8,128)(2,1)} async-done(((bf16[256,512]{1,0:T(8,128)(2,1)}), bf16[256,4096]{1,0:T(8,128)(2,1)}) %all-gather.15.cloned.1.call-update) | async-done | bytes 2097168 | tf_op jit(solution)/shard_map/all_gather | solution.py:66
  262.1 4.8 %fusion.6 = bf16[256,512]{1,0:T(8,128)(2,1)} fusion(f32[256,512]{1,0:T(8,128)S(1)} %fusion.14, bf16[256,4096]{1,0:T(8,128)(2,1)} %all-gather.15.cloned.1.call-done, bf16[4096,512]{1,0:T(8,128)(2,1)} %all-gather.17.cloned.1.call-done, f32[]{:T(128)} %bitcast.21, s32[512]{0:T(512)S(1)} %iota_add_fusion, s32[256]{0:T(256)S(1)} %iota_add_fusion.1), kind=kOutput, calls=%fused_computation.15 | convolution fusion | flops 1074397184 | bytes 7080964 | tf_op jit(solution)/shard_map/dot_general | solution.py:21
  266.8 0.0 all-gather.19.cloned.1.call-update
  266.9 0.0 all-gather.21.cloned.1.call-start
  266.9 0.7 all-gather.21.cloned.1.call-update
  267.6 0.0 all-gather.23.cloned.1.call-start
  267.7 40.0 %all-gather.19.cloned.1.call-done = bf16[256,4096]{1,0:T(8,128)(2,1)} async-done(((bf16[256,512]{1,0:T(8,128)(2,1)}), bf16[256,4096]{1,0:T(8,128)(2,1)}) %all-gather.19.cloned.1.call-update) | async-done | bytes 2097168 | tf_op jit(solution)/shard_map/all_gather | solution.py:73
  307.6 63.2 %all-gather.21.cloned.1.call-done = bf16[4096,512]{1,0:T(8,128)(2,1)} async-done(((bf16[256,512]{1,0:T(8,128)(2,1)}), bf16[4096,512]{1,0:T(8,128)(2,1)}) %all-gather.21.cloned.1.call-update) | async-done | bytes 4194320 | tf_op jit(solution)/shard_map/all_gather | solution.py:74
  370.8 4.8 %fusion.13 = bf16[256,512]{1,0:T(8,128)(2,1)} fusion(f32[256,512]{1,0:T(8,128)S(1)} %fusion.14, bf16[256,4096]{1,0:T(8,128)(2,1)} %all-gather.19.cloned.1.call-done, bf16[4096,512]{1,0:T(8,128)(2,1)} %all-gather.21.cloned.1.call-done), kind=kOutput, calls=%fused_computation.22 | convolution fusion | flops 1074003968 | bytes 7077888 | tf_op jit(solution)/shard_map/dot_general | solution.py:21
  375.6 0.0 all-gather.23.cloned.1.call-update
  375.6 4.2 fusion.7
  379.9 48.6 %all-gather.23.cloned.1.call-done = bf16[4096,512]{1,0:T(8,128)(2,1)} async-done(((bf16[256,512]{1,0:T(8,128)(2,1)}), bf16[4096,512]{1,0:T(8,128)(2,1)}) %all-gather.23.cloned.1.call-update) | async-done | bytes 4194320 | tf_op jit(solution)/shard_map/all_gather | solution.py:76
  428.5 4.8 %fusion.8 = bf16[256,512]{1,0:T(8,128)(2,1)} fusion(bf16[256,4096]{1,0:T(8,128)(2,1)} %all-gather.19.cloned.1.call-done, bf16[4096,512]{1,0:T(8,128)(2,1)} %all-gather.23.cloned.1.call-done, bf16[256,512]{1,0:T(8,128)(2,1)S(1)} %copy-done.1), kind=kOutput, calls=%fused_computation.17 | convolution fusion | flops 1074397184 | bytes 6815744 | tf_op jit(solution)/shard_map/dot_general | solution.py:21
  (10 shorter events, 0.0 us)
Async XLA Ops:
  7.2 42.6 %all-gather.9.cloned.1.call-start = ((), (), s32[]{:S(2)}) async-start(), calls=%async_computation.1 | async-start | bytes 2359296 | tf_op jit(solution)/shard_map/all_gather | solution.py:57
  10.5 102.4 %all-gather.11.cloned.1.call-start = ((), (), s32[]{:S(2)}) async-start(), calls=%async_computation.2 | async-start | bytes 4456448 | tf_op jit(solution)/shard_map/all_gather | solution.py:58
  13.7 158.0 %all-gather.13.cloned.1.call-start = ((), (), s32[]{:S(2)}) async-start(), calls=%async_computation.3 | async-start | bytes 4456448 | tf_op jit(solution)/shard_map/all_gather | solution.py:63
  14.5 212.3 %all-gather.17.cloned.1.call-start = ((), (), s32[]{:S(2)}) async-start(), calls=%async_computation.5 | async-start | bytes 4456448 | tf_op jit(solution)/shard_map/all_gather | solution.py:70
  117.0 5.7 %copy-start.2 = (s32[32,32]{1,0:T(8,128)S(1)}, s32[32,32]{1,0:T(8,128)}, u32[]{:S(2)}) copy-start(s32[32,32]{1,0:T(8,128)} %param.16) | copy-start | bytes 12292
  117.0 54.7 %copy-start = (bf16[256,512]{1,0:T(8,128)(2,1)S(1)}, bf16[256,512]{1,0:T(8,128)(2,1)}, u32[]{:S(2)}) copy-start(bf16[256,512]{1,0:T(8,128)(2,1)} %fusion.10) | copy-start | bytes 786436
  118.6 53.1 %all-to-all-start = ((bf16[8,256,512]{1,2,0:T(8,128)(2,1)}), bf16[8,256,512]{1,2,0:T(8,128)(2,1)S(1)}, u32[]{:S(2)}, u32[]{:S(2)}) async-start(bf16[8,256,512]{1,2,0:T(8,128)(2,1)} %stack.2), calls=%async_computation | async-start | bytes 4194304 | tf_op jit(solution)/shard_map/all_to_all | solution.py:61
  122.6 139.5 %all-gather.15.cloned.1.call-start = ((), (), s32[]{:S(2)}) async-start(), calls=%async_computation.4 | async-start | bytes 2359296 | tf_op jit(solution)/shard_map/all_gather | solution.py:66
  171.7 5.4 %copy-start.3 = (s32[32,32]{1,0:T(8,128)S(1)}, s32[32,32]{1,0:T(8,128)}, u32[]{:S(2)}) copy-start(s32[32,32]{1,0:T(8,128)} %param.17) | copy-start | bytes 12292
  176.4 131.3 %all-gather.19.cloned.1.call-start = ((), (), s32[]{:S(2)}) async-start(), calls=%async_computation.6 | async-start | bytes 2359296 | tf_op jit(solution)/shard_map/all_gather | solution.py:73
  266.8 108.8 %copy-start.4 = (bf16[256,4096]{1,0:T(8,128)(2,1)S(1)}, bf16[256,4096]{1,0:T(8,128)(2,1)}, u32[]{:S(2)}) copy-start(bf16[256,4096]{1,0:T(8,128)(2,1)} %all-gather.15.cloned.1.call-done) | copy-start | bytes 6291460
  266.9 103.9 %all-gather.21.cloned.1.call-start = ((), (), s32[]{:S(2)}) async-start(), calls=%async_computation.7 | async-start | bytes 4456448 | tf_op jit(solution)/shard_map/all_gather | solution.py:74
  267.6 160.9 %all-gather.23.cloned.1.call-start = ((), (), s32[]{:S(2)}) async-start(), calls=%async_computation.8 | async-start | bytes 4456448 | tf_op jit(solution)/shard_map/all_gather | solution.py:76
  375.6 52.9 %copy-start.1 = (bf16[256,512]{1,0:T(8,128)(2,1)S(1)}, bf16[256,512]{1,0:T(8,128)(2,1)}, u32[]{:S(2)}) copy-start(bf16[256,512]{1,0:T(8,128)(2,1)} %fusion.6) | copy-start | bytes 786436
Sparse Core Ops, SparseCore 0:
  10.6 39.0 all-gather.8
  52.8 60.0 all-gather.10
  115.9 55.6 all-gather.12
  174.0 52.6 all-gather.16
  228.8 33.2 all-gather.14
  267.0 40.5 all-gather.18
  310.7 60.0 all-gather.20
  375.7 52.6 all-gather.22
